TPU v7x, 128 devices: a whole 4x4x4 slice. The times are simulated.
128 devices in a mesh: row: 8 (over z, core), col: 16 (over y, x).
Axes of the slice: x: 4, y: 4, z: 4, core: 2. Of those that a mesh axis runs over, the one named last changes fastest.
Arguments:
- hidden: bfloat16 [1408, 16384], P('col', 'row'), may hold values from -18 to 18
- gain_in: bfloat16 [1408], replicated, may hold values from 0.5 to 1.5
- w_query: bfloat16 [1408, 1408], P('col'), may hold values from -0.3125 to 0.3125
- w_pair: bfloat16 [2, 1408, 1408], P(None, 'col'), may hold values from -0.15625 to 0.15625
- kv_cache: bfloat16 [2, 1408, 16384], P(None, 'col', 'row'), may hold values from -103 to 103
- recompute_rows: int32 [8, 200], P('row'), may hold values from 0 to 2047, as said below
- segment_ids: int32 [16384], P('row'), may hold values from -1 to 1, as said below
- w_out: bfloat16 [1408, 1408], P('col'), may hold values from -0.3125 to 0.3125
- gain_merge: bfloat16 [1408], replicated, may hold values from 0.5 to 1.5
- w_merge: bfloat16 [4, 1408, 1408], P(None, 'col'), may hold values from -0.078125 to 0.078125
- requests: int32 [8, 16, 85], P('row'), may hold values from -1 to 511, as said below
Outputs:
- delivered: bfloat16 [8, 16, 85, 1408], P('row', 'col')
Inputs may be any that keep to these rules, and one draw needn't show every extreme that they name: `segment_ids`: ids do not fall along the tokens except to -1 for the padding at the end; every image covers a multiple of 4 tokens and starts at a multiple of 4. `recompute_rows`: the 200 offsets of one index of row are distinct. `requests`: for each index of row, the lists of all owners together name each of its 512 merged tokens exactly once; unused slots hold -1 and follow the used ones.
All inputs are finite; a program needn't handle non-finite values.
Results may differ from a plain program's by a relative error of at most 0.025.
The roundings to bfloat16 on the way count: a program that leaves them out, or rounds other values in their place, can miss the bound.
Values may be sent and summed in bfloat16 or wider, within the bound.
A program may use at most 128 MiB of HBM per device.

v0:
```python
import jax
import jax.numpy as jnp
from jax import lax
from jax.sharding import PartitionSpec as P

HD = 88
EPSILON = 1e-06
MASKED = -1e30
KEY_BLOCK = 1024


def on_device(
    hidden,
    gain_in,
    w_query,
    w_pair,
    kv_cache,
    recompute_rows,
    segment_ids,
    w_out,
    gain_merge,
    w_merge,
    requests,
):
    local_width, tok_rows = hidden.shape
    model_width = w_query.shape[1]
    n_col = model_width // local_width
    heads_here = local_width // HD
    score_scale = HD ** (-0.5)
    col_index = lax.axis_index("col")
    full_rows = lax.all_gather(hidden, "col", axis=0, tiled=True)
    out_weight = lax.all_gather(w_out, "col", axis=0, tiled=True)
    full_float = full_rows.astype(jnp.float32)
    in_mean = jnp.sum(full_float, axis=0, keepdims=True) / model_width
    in_square = jnp.sum(full_float * full_float, axis=0, keepdims=True) / model_width
    normed = (
        (full_float - in_mean)
        * lax.rsqrt(in_square - in_mean * in_mean + EPSILON)
        * gain_in.astype(jnp.float32)[:, None]
    ).astype(jnp.bfloat16)
    queries = jnp.dot(w_query, normed, preferred_element_type=jnp.float32).astype(jnp.bfloat16)
    picked_rows = recompute_rows[0]
    normed_picked = jnp.take(normed, picked_rows, axis=1)
    fresh_pairs = jnp.dot(
        w_pair.reshape(2 * local_width, model_width),
        normed_picked,
        preferred_element_type=jnp.float32,
    )
    fresh_pairs = fresh_pairs.astype(jnp.bfloat16).reshape(2, local_width, -1)
    keys_values = kv_cache.at[:, :, picked_rows].set(fresh_pairs)
    query_heads = queries.reshape(heads_here, HD, tok_rows)
    pair_local = jnp.concatenate(
        [keys_values.reshape(2 * local_width, tok_rows), segment_ids.astype(jnp.bfloat16)[None, :]],
        axis=0,
    )
    pair_all = lax.all_gather(pair_local, "row", axis=1, tiled=True)
    pair_rows = pair_all[: 2 * local_width].reshape(2, local_width, -1)
    segment_line = pair_all[2 * local_width].astype(jnp.int32)

    def take_block(carried, pair_block, segment_block):
        running_max, running_sum, weighted = carried
        key_block = pair_block[0].reshape(heads_here, HD, -1)
        value_block = pair_block[1].reshape(heads_here, HD, -1)
        scores = (
            jnp.einsum("hdq,hdk->hqk", query_heads, key_block, preferred_element_type=jnp.float32)
            * score_scale
        )
        allowed = (segment_ids[:, None] == segment_block[None, :])[None, :, :]
        new_max = jnp.maximum(running_max, jnp.max(jnp.where(allowed, scores, MASKED), axis=2))
        weights_exp = jnp.where(allowed, jnp.exp(scores - new_max[:, :, None]), 0.0)
        factor = jnp.exp(running_max - new_max)
        running_sum = running_sum * factor + jnp.sum(weights_exp, axis=2)
        product = jnp.einsum(
            "hqk,hdk->hdq",
            weights_exp.astype(jnp.bfloat16),
            value_block,
            preferred_element_type=jnp.float32,
        )
        weighted = weighted * factor[:, None, :] + product
        return (new_max, running_sum, weighted)

    starting = (
        jnp.full((heads_here, tok_rows), MASKED, jnp.float32),
        jnp.zeros((heads_here, tok_rows), jnp.float32),
        jnp.zeros((heads_here, HD, tok_rows), jnp.float32),
    )
    piece_rows = pair_rows.shape[2]
    whole_blocks = piece_rows // KEY_BLOCK

    def loop_body(block_index, loop_state):
        pair_block = lax.dynamic_slice_in_dim(pair_rows, block_index * KEY_BLOCK, KEY_BLOCK, 2)
        segment_block = lax.dynamic_slice_in_dim(
            segment_line, block_index * KEY_BLOCK, KEY_BLOCK, 0
        )
        return take_block(loop_state, pair_block, segment_block)

    running_max, running_sum, weighted = lax.fori_loop(0, whole_blocks, loop_body, starting)
    attended = (
        (weighted / running_sum[:, None, :]).astype(jnp.bfloat16).reshape(local_width, tok_rows)
    )
    chunk = tok_rows // n_col
    attended_chunk = lax.all_to_all(attended, "col", 1, 0, tiled=True)
    x_chunk = lax.dynamic_slice_in_dim(full_float, col_index * chunk, chunk, 1)
    projected = lax.dot_general(
        out_weight, attended_chunk, (((0,), (0,)), ((), ())), preferred_element_type=jnp.float32
    )
    updated = x_chunk + projected
    row_mean = jnp.sum(updated, axis=0, keepdims=True) / model_width
    row_square = jnp.sum(updated * updated, axis=0, keepdims=True) / model_width
    merger_chunk = (
        (updated - row_mean)
        * lax.rsqrt(row_square - row_mean * row_mean + EPSILON)
        * gain_merge.astype(jnp.float32)[:, None]
    ).astype(jnp.bfloat16)
    merge_weight, _ = lax.optimization_barrier((w_merge, pair_all))
    merge_full = lax.all_gather(merge_weight, "col", axis=1, tiled=True)
    grouped = merger_chunk.reshape(model_width, chunk // 4, 4)
    merged_here = jnp.einsum("fgi,ifd->gd", grouped, merge_full, preferred_element_type=jnp.float32)
    merged_all = lax.all_gather(merged_here.astype(jnp.bfloat16), "col", axis=0, tiled=True)
    wanted_rows = lax.dynamic_index_in_dim(requests[0], col_index, 0, keepdims=False)
    is_valid = wanted_rows >= 0
    safe_index = jnp.where(is_valid, wanted_rows, 0)
    picked = jnp.where(is_valid[:, None], merged_all[safe_index], jnp.zeros((), jnp.bfloat16))
    return picked.reshape(1, 1, picked.shape[0], model_width)


def solution(mesh):
    placed = (
        P("col", "row"),
        P(),
        P("col", None),
        P(None, "col", None),
        P(None, "col", "row"),
        P("row", None),
        P("row"),
        P("col", None),
        P(),
        P(None, "col", None),
        P("row", None, None),
    )
    return jax.shard_map(
        on_device,
        mesh=mesh,
        in_specs=placed,
        out_specs=P("row", "col", None, None),
        check_vma=False,
    )
```

profile of v0, /device:TPU:0, one launch (start us, length us, event | category | flops | bytes accessed | tf_op | source)
XLA Modules:
  0.0 484.3 jit_solution(13265763063287293929)
XLA Ops:
  12.5 58.2 %all-gather.6.cloned.1.call-done = bf16[1408,2048]{1,0:T(8,128)(2,1)} async-done(((bf16[88,2048]{1,0:T(8,128)(2,1)}), bf16[1408,2048]{1,0:T(8,128)(2,1)}) %all-gather.6.cloned.1.call-update) | async-done | bytes 5767184 | tf_op jit(solution)/shard_map/all_gather | solution.py:31
  70.7 8.3 %copy.28 = bf16[1408,2048]{0,1:T(8,128)(2,1)} copy(bf16[1408,2048]{1,0:T(8,128)(2,1)} %all-gather.6.cloned.1.call-done) | data formatting | bytes 11534336 | tf_op jit(solution)/shard_map/all_gather | solution.py:31
  87.6 5.0 %gather_fusion = bf16[200,1408]{1,0:T(8,128)(2,1)S(1)} fusion(bf16[1408,2048]{0,1:T(8,128)(2,1)} %multiply_convert_fusion, s32[1024]{0:T(1024)S(1)} %pad_clamp_fusion.1), kind=kCustom, calls=%fused_computation | custom fusion | bytes 1127200 | tf_op jit(solution)/shard_map/jit(_take)/gather | solution.py:43
  93.2 6.9 %scatter_fusion = bf16[2,88,2048]{1,0,2:T(2,128)(2,1)S(1)} fusion(bf16[2,88,2048]{1,0,2:T(2,128)(2,1)S(1)} %copy.30, s32[200]{0:T(256)S(1)} %bitcast.122, bf16[200,2,88]{2,1,0:T(2,128)(2,1)S(1)} %bitcast.115), kind=kCustom, calls=%fused_computation.2 | custom fusion | bytes 212000 | tf_op jit(solution)/shard_map/scatter | solution.py:50
  107.5 34.2 %all-gather.8.cloned.1.call-done = bf16[177,16384]{1,0:T(8,128)(2,1)} async-done(((bf16[177,2048]{1,0:T(8,128)(2,1)}), bf16[177,16384]{1,0:T(8,128)(2,1)}) %all-gather.8.cloned.1.call-update) | async-done | bytes 5799952 | tf_op jit(solution)/shard_map/all_gather | solution.py:56
  141.7 5.8 %slice.29 = bf16[176,16384]{1,0:T(8,128)(2,1)} slice(bf16[177,16384]{1,0:T(8,128)(2,1)} %all-gather.8.cloned.1.call-done), slice={[0:176], [0:16384]} | slice | bytes 11534336 | tf_op jit(solution)/shard_map/slice | solution.py:57
  148.5 254.0 %while.18 = (s32[]{:T(128)}, f32[1,2048]{1,0:T(1,128)S(1)}, f32[1,2048]{1,0:T(1,128)S(1)}, f32[1,88,2048]{2,1,0:T(8,128)S(1)}, s32[2048]{0:T(1024)S(1)}, /*index...) while((s32[]{:T(128)}, f32[1,2048]{1,0:T(1,128)S(1)}, ...), condition=%wide.region_6.7_spmd.clone, body=%wide.region_3.0_spmd.clone.sunk | while | flops 768108544 | bytes 27504848 | solution.py:97
  148.5 5.6 %fusion.45 = (f32[2048]{0:T(1024)S(1)}, f32[1024,2048]{1,0:T(8,128)}) fusion(s32[2048]{0:T(1024)S(1)} %get-tuple-element.292, s32[1024]{0:T(1024)S(1)} %dynamic_slice.32, bf16[1,88,2048]{2,1,0:T(8,128)(2,1)S(1)} %get-tuple-element.295, bf16[2,88,16384]{2,1,0:T(8,128)(2,1)} %get-tuple-element.294, s32[]{:T(128)S(6)} %select_n.132), kind=kOutput, calls=%fused_computation.5.clone.1 | convolution fusion | flops 377485312 | bytes 8949764 | tf_op jit(solution)/shard_map/while/body/eval_jaxpr/hdq,hdk->hqk/dot_general | solution.py:65
  158.8 5.5 %fusion.49 = f32[1,88,2048]{2,1,0:T(8,128)S(1)} fusion(f32[1024,2048]{1,0:T(8,128)} %get-tuple-element.259, f32[2048]{0:T(1024)S(1)} %bitcast.110, s32[2048]{0:T(1024)S(1)} %get-tuple-element.292, s32[1024]{0:T(1024)S(1)} %dynamic_slice.32, f32[1,88,2048]{2,1,0:T(8,128)S(1)} %get-tuple-element.278, f32[2048]{0:T(1024)S(1)} %bitcast.117, ...), kind=kOutput, calls=%fused_computation.12.clone.1 | convolution fusion | flops 380125184 | bytes 10039305 | tf_op jit(solution)/shard_map/while/body/eval_jaxpr/hqk,hdk->hdq/dot_general | solution.py:73
  164.3 5.6 %fusion.45 = (f32[2048]{0:T(1024)S(1)}, f32[1024,2048]{1,0:T(8,128)}) fusion(s32[2048]{0:T(1024)S(1)} %get-tuple-element.292, s32[1024]{0:T(1024)S(1)} %dynamic_slice.32, bf16[1,88,2048]{2,1,0:T(8,128)(2,1)S(1)} %get-tuple-element.295, bf16[2,88,16384]{2,1,0:T(8,128)(2,1)} %get-tuple-element.294, s32[]{:T(128)S(6)} %select_n.132), kind=kOutput, calls=%fused_computation.5.clone.1 | convolution fusion | flops 377485312 | bytes 8949764 | tf_op jit(solution)/shard_map/while/body/eval_jaxpr/hdq,hdk->hqk/dot_general | solution.py:65
  174.5 5.4 %fusion.49 = f32[1,88,2048]{2,1,0:T(8,128)S(1)} fusion(f32[1024,2048]{1,0:T(8,128)} %get-tuple-element.259, f32[2048]{0:T(1024)S(1)} %bitcast.110, s32[2048]{0:T(1024)S(1)} %get-tuple-element.292, s32[1024]{0:T(1024)S(1)} %dynamic_slice.32, f32[1,88,2048]{2,1,0:T(8,128)S(1)} %get-tuple-element.278, f32[2048]{0:T(1024)S(1)} %bitcast.117, ...), kind=kOutput, calls=%fused_computation.12.clone.1 | convolution fusion | flops 380125184 | bytes 10039305 | tf_op jit(solution)/shard_map/while/body/eval_jaxpr/hqk,hdk->hdq/dot_general | solution.py:73
  180.0 5.6 %fusion.45 = (f32[2048]{0:T(1024)S(1)}, f32[1024,2048]{1,0:T(8,128)}) fusion(s32[2048]{0:T(1024)S(1)} %get-tuple-element.292, s32[1024]{0:T(1024)S(1)} %dynamic_slice.32, bf16[1,88,2048]{2,1,0:T(8,128)(2,1)S(1)} %get-tuple-element.295, bf16[2,88,16384]{2,1,0:T(8,128)(2,1)} %get-tuple-element.294, s32[]{:T(128)S(6)} %select_n.132), kind=kOutput, calls=%fused_computation.5.clone.1 | convolution fusion | flops 377485312 | bytes 8949764 | tf_op jit(solution)/shard_map/while/body/eval_jaxpr/hdq,hdk->hqk/dot_general | solution.py:65
  185.6 4.7 fusion.47
  190.4 5.4 %fusion.49 = f32[1,88,2048]{2,1,0:T(8,128)S(1)} fusion(f32[1024,2048]{1,0:T(8,128)} %get-tuple-element.259, f32[2048]{0:T(1024)S(1)} %bitcast.110, s32[2048]{0:T(1024)S(1)} %get-tuple-element.292, s32[1024]{0:T(1024)S(1)} %dynamic_slice.32, f32[1,88,2048]{2,1,0:T(8,128)S(1)} %get-tuple-element.278, f32[2048]{0:T(1024)S(1)} %bitcast.117, ...), kind=kOutput, calls=%fused_computation.12.clone.1 | convolution fusion | flops 380125184 | bytes 10039305 | tf_op jit(solution)/shard_map/while/body/eval_jaxpr/hqk,hdk->hdq/dot_general | solution.py:73
  195.8 5.6 %fusion.45 = (f32[2048]{0:T(1024)S(1)}, f32[1024,2048]{1,0:T(8,128)}) fusion(s32[2048]{0:T(1024)S(1)} %get-tuple-element.292, s32[1024]{0:T(1024)S(1)} %dynamic_slice.32, bf16[1,88,2048]{2,1,0:T(8,128)(2,1)S(1)} %get-tuple-element.295, bf16[2,88,16384]{2,1,0:T(8,128)(2,1)} %get-tuple-element.294, s32[]{:T(128)S(6)} %select_n.132), kind=kOutput, calls=%fused_computation.5.clone.1 | convolution fusion | flops 377485312 | bytes 8949764 | tf_op jit(solution)/shard_map/while/body/eval_jaxpr/hdq,hdk->hqk/dot_general | solution.py:65
  206.0 5.9 %fusion.49 = f32[1,88,2048]{2,1,0:T(8,128)S(1)} fusion(f32[1024,2048]{1,0:T(8,128)} %get-tuple-element.259, f32[2048]{0:T(1024)S(1)} %bitcast.110, s32[2048]{0:T(1024)S(1)} %get-tuple-element.292, s32[1024]{0:T(1024)S(1)} %dynamic_slice.32, f32[1,88,2048]{2,1,0:T(8,128)S(1)} %get-tuple-element.278, f32[2048]{0:T(1024)S(1)} %bitcast.117, ...), kind=kOutput, calls=%fused_computation.12.clone.1 | convolution fusion | flops 380125184 | bytes 10039305 | tf_op jit(solution)/shard_map/while/body/eval_jaxpr/hqk,hdk->hdq/dot_general | solution.py:73
  212.0 5.6 %fusion.45 = (f32[2048]{0:T(1024)S(1)}, f32[1024,2048]{1,0:T(8,128)}) fusion(s32[2048]{0:T(1024)S(1)} %get-tuple-element.292, s32[1024]{0:T(1024)S(1)} %dynamic_slice.32, bf16[1,88,2048]{2,1,0:T(8,128)(2,1)S(1)} %get-tuple-element.295, bf16[2,88,16384]{2,1,0:T(8,128)(2,1)} %get-tuple-element.294, s32[]{:T(128)S(6)} %select_n.132), kind=kOutput, calls=%fused_computation.5.clone.1 | convolution fusion | flops 377485312 | bytes 8949764 | tf_op jit(solution)/shard_map/while/body/eval_jaxpr/hdq,hdk->hqk/dot_general | solution.py:65
  217.5 4.7 fusion.47
  222.3 5.4 %fusion.49 = f32[1,88,2048]{2,1,0:T(8,128)S(1)} fusion(f32[1024,2048]{1,0:T(8,128)} %get-tuple-element.259, f32[2048]{0:T(1024)S(1)} %bitcast.110, s32[2048]{0:T(1024)S(1)} %get-tuple-element.292, s32[1024]{0:T(1024)S(1)} %dynamic_slice.32, f32[1,88,2048]{2,1,0:T(8,128)S(1)} %get-tuple-element.278, f32[2048]{0:T(1024)S(1)} %bitcast.117, ...), kind=kOutput, calls=%fused_computation.12.clone.1 | convolution fusion | flops 380125184 | bytes 10039305 | tf_op jit(solution)/shard_map/while/body/eval_jaxpr/hqk,hdk->hdq/dot_general | solution.py:73
  227.8 5.6 %fusion.45 = (f32[2048]{0:T(1024)S(1)}, f32[1024,2048]{1,0:T(8,128)}) fusion(s32[2048]{0:T(1024)S(1)} %get-tuple-element.292, s32[1024]{0:T(1024)S(1)} %dynamic_slice.32, bf16[1,88,2048]{2,1,0:T(8,128)(2,1)S(1)} %get-tuple-element.295, bf16[2,88,16384]{2,1,0:T(8,128)(2,1)} %get-tuple-element.294, s32[]{:T(128)S(6)} %select_n.132), kind=kOutput, calls=%fused_computation.5.clone.1 | convolution fusion | flops 377485312 | bytes 8949764 | tf_op jit(solution)/shard_map/while/body/eval_jaxpr/hdq,hdk->hqk/dot_general | solution.py:65
  233.4 5.9 %fusion.47 = f32[2048]{0:T(1024)S(1)} fusion(f32[1024,2048]{1,0:T(8,128)} %get-tuple-element.259, f32[2048]{0:T(1024)S(1)} %bitcast.109, s32[2048]{0:T(1024)S(1)} %get-tuple-element.292, s32[1024]{0:T(1024)S(1)} %dynamic_slice.32), kind=kLoop, calls=%fused_computation.9.clone.1 | loop fusion | flops 10483712 | bytes 8417280 | tf_op jit(solution)/shard_map/while/body/eval_jaxpr/reduce_sum | solution.py:72
  239.3 5.4 %fusion.49 = f32[1,88,2048]{2,1,0:T(8,128)S(1)} fusion(f32[1024,2048]{1,0:T(8,128)} %get-tuple-element.259, f32[2048]{0:T(1024)S(1)} %bitcast.110, s32[2048]{0:T(1024)S(1)} %get-tuple-element.292, s32[1024]{0:T(1024)S(1)} %dynamic_slice.32, f32[1,88,2048]{2,1,0:T(8,128)S(1)} %get-tuple-element.278, f32[2048]{0:T(1024)S(1)} %bitcast.117, ...), kind=kOutput, calls=%fused_computation.12.clone.1 | convolution fusion | flops 380125184 | bytes 10039305 | tf_op jit(solution)/shard_map/while/body/eval_jaxpr/hqk,hdk->hdq/dot_general | solution.py:73
  244.8 5.6 %fusion.45 = (f32[2048]{0:T(1024)S(1)}, f32[1024,2048]{1,0:T(8,128)}) fusion(s32[2048]{0:T(1024)S(1)} %get-tuple-element.292, s32[1024]{0:T(1024)S(1)} %dynamic_slice.32, bf16[1,88,2048]{2,1,0:T(8,128)(2,1)S(1)} %get-tuple-element.295, bf16[2,88,16384]{2,1,0:T(8,128)(2,1)} %get-tuple-element.294, s32[]{:T(128)S(6)} %select_n.132), kind=kOutput, calls=%fused_computation.5.clone.1 | convolution fusion | flops 377485312 | bytes 8949764 | tf_op jit(solution)/shard_map/while/body/eval_jaxpr/hdq,hdk->hqk/dot_general | solution.py:65
  250.4 4.8 fusion.47
  255.2 5.7 %fusion.49 = f32[1,88,2048]{2,1,0:T(8,128)S(1)} fusion(f32[1024,2048]{1,0:T(8,128)} %get-tuple-element.259, f32[2048]{0:T(1024)S(1)} %bitcast.110, s32[2048]{0:T(1024)S(1)} %get-tuple-element.292, s32[1024]{0:T(1024)S(1)} %dynamic_slice.32, f32[1,88,2048]{2,1,0:T(8,128)S(1)} %get-tuple-element.278, f32[2048]{0:T(1024)S(1)} %bitcast.117, ...), kind=kOutput, calls=%fused_computation.12.clone.1 | convolution fusion | flops 380125184 | bytes 10039305 | tf_op jit(solution)/shard_map/while/body/eval_jaxpr/hqk,hdk->hdq/dot_general | solution.py:73
  261.0 5.6 %fusion.45 = (f32[2048]{0:T(1024)S(1)}, f32[1024,2048]{1,0:T(8,128)}) fusion(s32[2048]{0:T(1024)S(1)} %get-tuple-element.292, s32[1024]{0:T(1024)S(1)} %dynamic_slice.32, bf16[1,88,2048]{2,1,0:T(8,128)(2,1)S(1)} %get-tuple-element.295, bf16[2,88,16384]{2,1,0:T(8,128)(2,1)} %get-tuple-element.294, s32[]{:T(128)S(6)} %select_n.132), kind=kOutput, calls=%fused_computation.5.clone.1 | convolution fusion | flops 377485312 | bytes 8949764 | tf_op jit(solution)/shard_map/while/body/eval_jaxpr/hdq,hdk->hqk/dot_general | solution.py:65
  266.6 4.8 fusion.47
  271.4 5.7 %fusion.49 = f32[1,88,2048]{2,1,0:T(8,128)S(1)} fusion(f32[1024,2048]{1,0:T(8,128)} %get-tuple-element.259, f32[2048]{0:T(1024)S(1)} %bitcast.110, s32[2048]{0:T(1024)S(1)} %get-tuple-element.292, s32[1024]{0:T(1024)S(1)} %dynamic_slice.32, f32[1,88,2048]{2,1,0:T(8,128)S(1)} %get-tuple-element.278, f32[2048]{0:T(1024)S(1)} %bitcast.117, ...), kind=kOutput, calls=%fused_computation.12.clone.1 | convolution fusion | flops 380125184 | bytes 10039305 | tf_op jit(solution)/shard_map/while/body/eval_jaxpr/hqk,hdk->hdq/dot_general | solution.py:73
  277.1 5.6 %fusion.45 = (f32[2048]{0:T(1024)S(1)}, f32[1024,2048]{1,0:T(8,128)}) fusion(s32[2048]{0:T(1024)S(1)} %get-tuple-element.292, s32[1024]{0:T(1024)S(1)} %dynamic_slice.32, bf16[1,88,2048]{2,1,0:T(8,128)(2,1)S(1)} %get-tuple-element.295, bf16[2,88,16384]{2,1,0:T(8,128)(2,1)} %get-tuple-element.294, s32[]{:T(128)S(6)} %select_n.132), kind=kOutput, calls=%fused_computation.5.clone.1 | convolution fusion | flops 377485312 | bytes 8949764 | tf_op jit(solution)/shard_map/while/body/eval_jaxpr/hdq,hdk->hqk/dot_general | solution.py:65
  287.4 5.4 %fusion.49 = f32[1,88,2048]{2,1,0:T(8,128)S(1)} fusion(f32[1024,2048]{1,0:T(8,128)} %get-tuple-element.259, f32[2048]{0:T(1024)S(1)} %bitcast.110, s32[2048]{0:T(1024)S(1)} %get-tuple-element.292, s32[1024]{0:T(1024)S(1)} %dynamic_slice.32, f32[1,88,2048]{2,1,0:T(8,128)S(1)} %get-tuple-element.278, f32[2048]{0:T(1024)S(1)} %bitcast.117, ...), kind=kOutput, calls=%fused_computation.12.clone.1 | convolution fusion | flops 380125184 | bytes 10039305 | tf_op jit(solution)/shard_map/while/body/eval_jaxpr/hqk,hdk->hdq/dot_general | solution.py:73
  292.9 5.6 %fusion.45 = (f32[2048]{0:T(1024)S(1)}, f32[1024,2048]{1,0:T(8,128)}) fusion(s32[2048]{0:T(1024)S(1)} %get-tuple-element.292, s32[1024]{0:T(1024)S(1)} %dynamic_slice.32, bf16[1,88,2048]{2,1,0:T(8,128)(2,1)S(1)} %get-tuple-element.295, bf16[2,88,16384]{2,1,0:T(8,128)(2,1)} %get-tuple-element.294, s32[]{:T(128)S(6)} %select_n.132), kind=kOutput, calls=%fused_computation.5.clone.1 | convolution fusion | flops 377485312 | bytes 8949764 | tf_op jit(solution)/shard_map/while/body/eval_jaxpr/hdq,hdk->hqk/dot_general | solution.py:65
  303.1 5.4 %fusion.49 = f32[1,88,2048]{2,1,0:T(8,128)S(1)} fusion(f32[1024,2048]{1,0:T(8,128)} %get-tuple-element.259, f32[2048]{0:T(1024)S(1)} %bitcast.110, s32[2048]{0:T(1024)S(1)} %get-tuple-element.292, s32[1024]{0:T(1024)S(1)} %dynamic_slice.32, f32[1,88,2048]{2,1,0:T(8,128)S(1)} %get-tuple-element.278, f32[2048]{0:T(1024)S(1)} %bitcast.117, ...), kind=kOutput, calls=%fused_computation.12.clone.1 | convolution fusion | flops 380125184 | bytes 10039305 | tf_op jit(solution)/shard_map/while/body/eval_jaxpr/hqk,hdk->hdq/dot_general | solution.py:73
  308.6 5.6 %fusion.45 = (f32[2048]{0:T(1024)S(1)}, f32[1024,2048]{1,0:T(8,128)}) fusion(s32[2048]{0:T(1024)S(1)} %get-tuple-element.292, s32[1024]{0:T(1024)S(1)} %dynamic_slice.32, bf16[1,88,2048]{2,1,0:T(8,128)(2,1)S(1)} %get-tuple-element.295, bf16[2,88,16384]{2,1,0:T(8,128)(2,1)} %get-tuple-element.294, s32[]{:T(128)S(6)} %select_n.132), kind=kOutput, calls=%fused_computation.5.clone.1 | convolution fusion | flops 377485312 | bytes 8949764 | tf_op jit(solution)/shard_map/while/body/eval_jaxpr/hdq,hdk->hqk/dot_general | solution.py:65
  318.8 5.4 %fusion.49 = f32[1,88,2048]{2,1,0:T(8,128)S(1)} fusion(f32[1024,2048]{1,0:T(8,128)} %get-tuple-element.259, f32[2048]{0:T(1024)S(1)} %bitcast.110, s32[2048]{0:T(1024)S(1)} %get-tuple-element.292, s32[1024]{0:T(1024)S(1)} %dynamic_slice.32, f32[1,88,2048]{2,1,0:T(8,128)S(1)} %get-tuple-element.278, f32[2048]{0:T(1024)S(1)} %bitcast.117, ...), kind=kOutput, calls=%fused_computation.12.clone.1 | convolution fusion | flops 380125184 | bytes 10039305 | tf_op jit(solution)/shard_map/while/body/eval_jaxpr/hqk,hdk->hdq/dot_general | solution.py:73
  324.2 5.6 %fusion.45 = (f32[2048]{0:T(1024)S(1)}, f32[1024,2048]{1,0:T(8,128)}) fusion(s32[2048]{0:T(1024)S(1)} %get-tuple-element.292, s32[1024]{0:T(1024)S(1)} %dynamic_slice.32, bf16[1,88,2048]{2,1,0:T(8,128)(2,1)S(1)} %get-tuple-element.295, bf16[2,88,16384]{2,1,0:T(8,128)(2,1)} %get-tuple-element.294, s32[]{:T(128)S(6)} %select_n.132), kind=kOutput, calls=%fused_computation.5.clone.1 | convolution fusion | flops 377485312 | bytes 8949764 | tf_op jit(solution)/shard_map/while/body/eval_jaxpr/hdq,hdk->hqk/dot_general | solution.py:65
  334.4 5.4 %fusion.49 = f32[1,88,2048]{2,1,0:T(8,128)S(1)} fusion(f32[1024,2048]{1,0:T(8,128)} %get-tuple-element.259, f32[2048]{0:T(1024)S(1)} %bitcast.110, s32[2048]{0:T(1024)S(1)} %get-tuple-element.292, s32[1024]{0:T(1024)S(1)} %dynamic_slice.32, f32[1,88,2048]{2,1,0:T(8,128)S(1)} %get-tuple-element.278, f32[2048]{0:T(1024)S(1)} %bitcast.117, ...), kind=kOutput, calls=%fused_computation.12.clone.1 | convolution fusion | flops 380125184 | bytes 10039305 | tf_op jit(solution)/shard_map/while/body/eval_jaxpr/hqk,hdk->hdq/dot_general | solution.py:73
  339.9 5.6 %fusion.45 = (f32[2048]{0:T(1024)S(1)}, f32[1024,2048]{1,0:T(8,128)}) fusion(s32[2048]{0:T(1024)S(1)} %get-tuple-element.292, s32[1024]{0:T(1024)S(1)} %dynamic_slice.32, bf16[1,88,2048]{2,1,0:T(8,128)(2,1)S(1)} %get-tuple-element.295, bf16[2,88,16384]{2,1,0:T(8,128)(2,1)} %get-tuple-element.294, s32[]{:T(128)S(6)} %select_n.132), kind=kOutput, calls=%fused_computation.5.clone.1 | convolution fusion | flops 377485312 | bytes 8949764 | tf_op jit(solution)/shard_map/while/body/eval_jaxpr/hdq,hdk->hqk/dot_general | solution.py:65
  350.1 5.4 %fusion.49 = f32[1,88,2048]{2,1,0:T(8,128)S(1)} fusion(f32[1024,2048]{1,0:T(8,128)} %get-tuple-element.259, f32[2048]{0:T(1024)S(1)} %bitcast.110, s32[2048]{0:T(1024)S(1)} %get-tuple-element.292, s32[1024]{0:T(1024)S(1)} %dynamic_slice.32, f32[1,88,2048]{2,1,0:T(8,128)S(1)} %get-tuple-element.278, f32[2048]{0:T(1024)S(1)} %bitcast.117, ...), kind=kOutput, calls=%fused_computation.12.clone.1 | convolution fusion | flops 380125184 | bytes 10039305 | tf_op jit(solution)/shard_map/while/body/eval_jaxpr/hqk,hdk->hdq/dot_general | solution.py:73
  355.6 5.6 %fusion.45 = (f32[2048]{0:T(1024)S(1)}, f32[1024,2048]{1,0:T(8,128)}) fusion(s32[2048]{0:T(1024)S(1)} %get-tuple-element.292, s32[1024]{0:T(1024)S(1)} %dynamic_slice.32, bf16[1,88,2048]{2,1,0:T(8,128)(2,1)S(1)} %get-tuple-element.295, bf16[2,88,16384]{2,1,0:T(8,128)(2,1)} %get-tuple-element.294, s32[]{:T(128)S(6)} %select_n.132), kind=kOutput, calls=%fused_computation.5.clone.1 | convolution fusion | flops 377485312 | bytes 8949764 | tf_op jit(solution)/shard_map/while/body/eval_jaxpr/hdq,hdk->hqk/dot_general | solution.py:65
  365.8 5.4 %fusion.49 = f32[1,88,2048]{2,1,0:T(8,128)S(1)} fusion(f32[1024,2048]{1,0:T(8,128)} %get-tuple-element.259, f32[2048]{0:T(1024)S(1)} %bitcast.110, s32[2048]{0:T(1024)S(1)} %get-tuple-element.292, s32[1024]{0:T(1024)S(1)} %dynamic_slice.32, f32[1,88,2048]{2,1,0:T(8,128)S(1)} %get-tuple-element.278, f32[2048]{0:T(1024)S(1)} %bitcast.117, ...), kind=kOutput, calls=%fused_computation.12.clone.1 | convolution fusion | flops 380125184 | bytes 10039305 | tf_op jit(solution)/shard_map/while/body/eval_jaxpr/hqk,hdk->hdq/dot_general | solution.py:73
  371.2 5.6 %fusion.45 = (f32[2048]{0:T(1024)S(1)}, f32[1024,2048]{1,0:T(8,128)}) fusion(s32[2048]{0:T(1024)S(1)} %get-tuple-element.292, s32[1024]{0:T(1024)S(1)} %dynamic_slice.32, bf16[1,88,2048]{2,1,0:T(8,128)(2,1)S(1)} %get-tuple-element.295, bf16[2,88,16384]{2,1,0:T(8,128)(2,1)} %get-tuple-element.294, s32[]{:T(128)S(6)} %select_n.132), kind=kOutput, calls=%fused_computation.5.clone.1 | convolution fusion | flops 377485312 | bytes 8949764 | tf_op jit(solution)/shard_map/while/body/eval_jaxpr/hdq,hdk->hqk/dot_general | solution.py:65
  381.4 5.4 %fusion.49 = f32[1,88,2048]{2,1,0:T(8,128)S(1)} fusion(f32[1024,2048]{1,0:T(8,128)} %get-tuple-element.259, f32[2048]{0:T(1024)S(1)} %bitcast.110, s32[2048]{0:T(1024)S(1)} %get-tuple-element.292, s32[1024]{0:T(1024)S(1)} %dynamic_slice.32, f32[1,88,2048]{2,1,0:T(8,128)S(1)} %get-tuple-element.278, f32[2048]{0:T(1024)S(1)} %bitcast.117, ...), kind=kOutput, calls=%fused_computation.12.clone.1 | convolution fusion | flops 380125184 | bytes 10039305 | tf_op jit(solution)/shard_map/while/body/eval_jaxpr/hqk,hdk->hdq/dot_general | solution.py:73
  386.9 5.6 %fusion.45 = (f32[2048]{0:T(1024)S(1)}, f32[1024,2048]{1,0:T(8,128)}) fusion(s32[2048]{0:T(1024)S(1)} %get-tuple-element.292, s32[1024]{0:T(1024)S(1)} %dynamic_slice.32, bf16[1,88,2048]{2,1,0:T(8,128)(2,1)S(1)} %get-tuple-element.295, bf16[2,88,16384]{2,1,0:T(8,128)(2,1)} %get-tuple-element.294, s32[]{:T(128)S(6)} %select_n.132), kind=kOutput, calls=%fused_computation.5.clone.1 | convolution fusion | flops 377485312 | bytes 8949764 | tf_op jit(solution)/shard_map/while/body/eval_jaxpr/hdq,hdk->hqk/dot_general | solution.py:65
  397.1 5.4 %fusion.49 = f32[1,88,2048]{2,1,0:T(8,128)S(1)} fusion(f32[1024,2048]{1,0:T(8,128)} %get-tuple-element.259, f32[2048]{0:T(1024)S(1)} %bitcast.110, s32[2048]{0:T(1024)S(1)} %get-tuple-element.292, s32[1024]{0:T(1024)S(1)} %dynamic_slice.32, f32[1,88,2048]{2,1,0:T(8,128)S(1)} %get-tuple-element.278, f32[2048]{0:T(1024)S(1)} %bitcast.117, ...), kind=kOutput, calls=%fused_computation.12.clone.1 | convolution fusion | flops 380125184 | bytes 10039305 | tf_op jit(solution)/shard_map/while/body/eval_jaxpr/hqk,hdk->hdq/dot_general | solution.py:73
  403.5 6.1 %all-to-all-start = ((bf16[88,16,128]{2,0,1:T(8,128)(2,1)}), bf16[88,16,128]{2,0,1:T(8,128)(2,1)S(1)}, u32[]{:S(2)}, u32[]{:S(2)}) async-start(bf16[88,16,128]{2,0,1:T(8,128)(2,1)} %copy.32), calls=%async_computation | async-start | bytes 720896 | tf_op jit(solution)/shard_map/all_to_all | solution.py:102
  409.7 7.7 %convert_element_type.50 = f32[1408,2048]{0,1:T(8,128)} convert(bf16[1408,2048]{0,1:T(8,128)(2,1)} %copy.28) | non-fusion elementwise | flops 2883584 | bytes 17301504 | tf_op jit(solution)/shard_map/convert_element_type | solution.py:33
  423.1 8.8 %fusion.23 = bf16[32,1408]{1,0:T(8,128)(2,1)} fusion(bf16[4,1408,1408]{2,1,0:T(8,128)(2,1)} %all-gather.12.cloned.1.call-done, bf16[1408,32,4]{0,2,1:T(4,128)(2,1)S(1)} %reshape.212), kind=kOutput, calls=%fused_computation.36 | convolution fusion | flops 507555840 | bytes 16310272 | tf_op jit(solution)/shard_map/fgi,ifd->gd/dot_general | solution.py:118
  433.3 41.2 %all-gather.14.cloned.1.call-done = bf16[512,1408]{1,0:T(8,128)(2,1)} async-done(((bf16[32,1408]{1,0:T(8,128)(2,1)}), bf16[512,1408]{1,0:T(8,128)(2,1)}) %all-gather.14.cloned.1.call-update) | async-done | bytes 1441808 | tf_op jit(solution)/shard_map/all_gather | solution.py:119
  (132 shorter events, 86.3 us)
Async XLA Ops:
  6.5 86.1 %copy-start = (bf16[2,88,1408]{2,1,0:T(8,128)(2,1)S(1)}, bf16[2,88,1408]{2,1,0:T(8,128)(2,1)}, u32[]{:S(2)}) copy-start(bf16[2,88,1408]{2,1,0:T(8,128)(2,1)} %param.16) | copy-start | bytes 1486852
  6.5 64.2 %all-gather.6.cloned.1.call-start = ((), (), s32[]{:S(2)}) async-start(), calls=%async_computation.1 | async-start | bytes 6127616 | tf_op jit(solution)/shard_map/all_gather | solution.py:31
  7.3 134.4 %all-gather.8.cloned.1.call-start = ((), (), s32[]{:S(2)}) async-start(), calls=%async_computation.2 | async-start | bytes 6782976 | tf_op jit(solution)/shard_map/all_gather | solution.py:56
  79.1 4.5 copy-start.2
  87.6 15.2 %copy-start.4 = (bf16[88,1408]{1,0:T(8,128)(2,1)S(1)}, bf16[88,1408]{1,0:T(8,128)(2,1)}, u32[]{:S(2)}) copy-start(bf16[88,1408]{1,0:T(8,128)(2,1)} %param.15) | copy-start | bytes 743428
  101.8 315.6 %all-gather.10.cloned.1.call-start = ((), (), s32[]{:S(2)}) async-start(), calls=%async_computation.3 | async-start | bytes 4212736 | tf_op jit(solution)/shard_map/all_gather | solution.py:32
  102.5 320.5 %all-gather.12.cloned.1.call-start = ((), (), s32[]{:S(2)}) async-start(), calls=%async_computation.4 | async-start | bytes 16850944 | tf_op jit(solution)/shard_map/all_gather | solution.py:116
  102.8 45.7 %copy-start.3 = (s32[2048]{0:T(1024)S(1)}, s32[2048]{0:T(1024)}, u32[]{:S(2)}) copy-start(s32[2048]{0:T(1024)} %param.19) | copy-start | bytes 24580
  148.5 261.2 %copy-start.5 = (bf16[1408]{0:T(1024)(128)(2,1)S(1)}, bf16[1408]{0:T(1024)(128)(2,1)}, u32[]{:S(2)}) copy-start(bf16[1408]{0:T(1024)(128)(2,1)} %param.21) | copy-start | bytes 8452
  403.5 16.0 %all-to-all-start = ((bf16[88,16,128]{2,0,1:T(8,128)(2,1)}), bf16[88,16,128]{2,0,1:T(8,128)(2,1)S(1)}, u32[]{:S(2)}, u32[]{:S(2)}) async-start(bf16[88,16,128]{2,0,1:T(8,128)(2,1)} %copy.32), calls=%async_computation | async-start | bytes 720896 | tf_op jit(solution)/shard_map/all_to_all | solution.py:102
  409.6 64.9 %all-gather.14.cloned.1.call-start = ((), (), s32[]{:S(2)}) async-start(), calls=%async_computation.5 | async-start | bytes 1531904 | tf_op jit(solution)/shard_map/all_gather | solution.py:119
  422.9 54.9 %copy-start.1 = (bf16[2,88,1408]{2,1,0:T(8,128)(2,1)S(1)}, bf16[2,88,1408]{2,1,0:T(8,128)(2,1)}, u32[]{:S(2)}) copy-start(bf16[2,88,1408]{2,1,0:T(8,128)(2,1)} %param.16) | copy-start | bytes 1486852
Sparse Core Ops, SparseCore 0:
  9.5 61.1 all-gather.5
  101.9 39.7 all-gather.7
  143.8 50.4 all-gather.9
  196.4 106.0 all-gather.11
  432.0 42.4 all-gather.13
where the time goes:
time: 486 us; the launch traced here: 484 us
  matrix products  194 us (40%)
  waiting for transfers between devices  137 us (28%)
  other arithmetic  99.7 us (21%)
  local copies, waits for them, and re-layouts  33 us (7%)
  between operations  13.4 us (3%)
  starting transfers between devices  6.4 us (1%)
    dot_general x16, matrix products, take_block(): jnp.einsum('hdq,hdk->hqk', query_heads, key_block, preferred_element_type...  89.1 us
    dot_general x16, matrix products, take_block(): jnp.einsum('hqk,hdk->hdq', weights_exp.astype(jnp.bfloat16), value_block,...  87.5 us
    reduce_sum x16, other arithmetic, take_block(): running_sum = running_sum * factor + jnp.sum(weights_exp, axis=2)  75.4 us
    all_gather x1, waiting for transfers between devices, on_device(): full_rows = lax.all_gather(hidden, 'col', axis=0, tiled=True)  58.2 us
    all_gather x1, waiting for transfers between devices, on_device(): lax.all_gather(merged_here.astype(jnp.bfloat16), 'col', axis=0, tiled=True)  41.2 us
    all_gather x1, waiting for transfers between devices, on_device(): pair_all = lax.all_gather(pair_local, 'row', axis=1, tiled=True)  34.2 us
  transfers between devices with their start and end apart: 6, of which 4 were waited for; matrix products, arithmetic and copies ran while one was open for 58% of the time, Pallas kernels for 0%

commit v1 on v0

--- a/solution.py
+++ b/solution.py
@@ -28,8 +28,11 @@
     heads_here = local_width // HD
     score_scale = HD ** (-0.5)
     col_index = lax.axis_index("col")
-    full_rows = lax.all_gather(hidden, "col", axis=0, tiled=True)
-    out_weight = lax.all_gather(w_out, "col", axis=0, tiled=True)
+    full_rows, out_weight = jnp.split(
+        lax.all_gather(jnp.concatenate([hidden, w_out], axis=1), "col", axis=0, tiled=True),
+        [hidden.shape[1]],
+        axis=1,
+    )
     full_float = full_rows.astype(jnp.float32)
     in_mean = jnp.sum(full_float, axis=0, keepdims=True) / model_width
     in_square = jnp.sum(full_float * full_float, axis=0, keepdims=True) / model_width

time: 486 us -> 509 us (1.047)
  waiting for transfers between devices: 137 us -> 154 us
  local copies, waits for them, and re-layouts: 33 us -> 39 us
    all_gather x2 -> x1, waiting for transfers between devices: 58.3 us -> 75.2 us  [on_device(): lax.all_gather(jnp.concatenate([hidden, w_out], axis=1), 'col', axis=0, t...]
    unnamed x14 -> x15, local copies, waits for them, and re-layouts: 2.47 us -> 10.9 us
    all_gather x1 -> x0, local copies, waits for them, and re-layouts: 8.33 us -> none  [on_device(): full_rows = lax.all_gather(hidden, 'col', axis=0, tiled=True)]
    split x0 -> x1, local copies, waits for them, and re-layouts: none -> 6.03 us  [on_device(): jnp.split(lax.all_gather(jnp.concatenate([hidden, w_out], axis=1), 'col',...]
  transfers between devices with their start and end apart: 6 -> 5, of which waited for: 4 -> 4; matrix products, arithmetic and copies ran while one was open for 58% -> 55% of each run, Pallas kernels for 0% -> 0%
where the time goes in v1:
time: 509 us; the launch traced here: 508 us
  matrix products  194 us (38%)
  waiting for transfers between devices  154 us (30%)
  other arithmetic  100 us (20%)
  local copies, waits for them, and re-layouts  39 us (8%)
  between operations  13.4 us (3%)
  starting transfers between devices  6.72 us (1%)
    dot_general x16, matrix products, take_block(): jnp.einsum('hdq,hdk->hqk', query_heads, key_block, preferred_element_type...  89.2 us
    dot_general x16, matrix products, take_block(): jnp.einsum('hqk,hdk->hdq', weights_exp.astype(jnp.bfloat16), value_block,...  87.3 us
    all_gather x1, waiting for transfers between devices, on_device(): lax.all_gather(jnp.concatenate([hidden, w_out], axis=1), 'col', axis=0, t...  75.2 us
    reduce_sum x16, other arithmetic, take_block(): running_sum = running_sum * factor + jnp.sum(weights_exp, axis=2)  74.2 us
    all_gather x1, waiting for transfers between devices, on_device(): lax.all_gather(merged_here.astype(jnp.bfloat16), 'col', axis=0, tiled=True)  41.4 us
    all_gather x1, waiting for transfers between devices, on_device(): pair_all = lax.all_gather(pair_local, 'row', axis=1, tiled=True)  35 us
    unnamed x15, local copies, waits for them, and re-layouts  10.9 us
  transfers between devices with their start and end apart: 5, of which 4 were waited for; matrix products, arithmetic and copies ran while one was open for 55% of the time, Pallas kernels for 0%

profile of v1, /device:TPU:0, one launch (start us, length us, event | category | flops | bytes accessed | tf_op | source)
XLA Modules:
  0.0 507.6 jit_solution(5871661828501224413)
XLA Ops:
  13.8 75.2 %all-gather.5.cloned.1.call-done = bf16[1408,3456]{1,0:T(8,128)(2,1)} async-done(((bf16[88,3456]{1,0:T(8,128)(2,1)}), bf16[1408,3456]{1,0:T(8,128)(2,1)}) %all-gather.5.cloned.1.call-update) | async-done | bytes 9732112 | tf_op jit(solution)/shard_map/all_gather | solution.py:32
  89.0 6.0 %split.8 = bf16[1408,2048]{1,0:T(8,128)(2,1)} slice(bf16[1408,3456]{1,0:T(8,128)(2,1)} %all-gather.5.cloned.1.call-done), slice={[0:1408], [0:2048]} | slice | bytes 11534336 | tf_op jit(solution)/shard_map/split | solution.py:31
  95.1 8.4 %copy.37 = bf16[1408,2048]{0,1:T(8,128)(2,1)} copy(bf16[1408,2048]{1,0:T(8,128)(2,1)} %split.8) | data formatting | bytes 11534336
  111.9 5.0 gather_fusion
  117.5 6.9 %scatter_fusion = bf16[2,88,2048]{1,0,2:T(2,128)(2,1)S(1)} fusion(bf16[2,88,2048]{1,0,2:T(2,128)(2,1)S(1)} %copy.33, s32[200]{0:T(256)S(1)} %bitcast.117, bf16[200,2,88]{2,1,0:T(2,128)(2,1)S(1)} %bitcast.109), kind=kCustom, calls=%fused_computation.2 | custom fusion | bytes 212000 | tf_op jit(solution)/shard_map/scatter | solution.py:53
  126.4 4.7 fusion.26
  131.1 35.0 %all-gather.7.cloned.1.call-done = bf16[177,16384]{1,0:T(8,128)(2,1)} async-done(((bf16[177,2048]{1,0:T(8,128)(2,1)}), bf16[177,16384]{1,0:T(8,128)(2,1)}) %all-gather.7.cloned.1.call-update) | async-done | bytes 5799952 | tf_op jit(solution)/shard_map/all_gather | solution.py:59
  166.0 5.7 %slice.29 = bf16[176,16384]{1,0:T(8,128)(2,1)} slice(bf16[177,16384]{1,0:T(8,128)(2,1)} %all-gather.7.cloned.1.call-done), slice={[0:176], [0:16384]} | slice | bytes 11534336 | tf_op jit(solution)/shard_map/slice | solution.py:60
  172.8 252.6 %while.18 = (s32[]{:T(128)}, f32[1,2048]{1,0:T(1,128)S(1)}, f32[1,2048]{1,0:T(1,128)S(1)}, f32[1,88,2048]{2,1,0:T(8,128)S(1)}, s32[2048]{0:T(1024)S(1)}, /*index...) while((s32[]{:T(128)}, f32[1,2048]{1,0:T(1,128)S(1)}, ...), condition=%wide.region_6.7_spmd.clone, body=%wide.region_3.0_spmd.clone.sunk | while | flops 768108544 | bytes 27504848 | solution.py:100
  172.8 5.7 %fusion.48 = (f32[2048]{0:T(1024)S(1)}, f32[1024,2048]{1,0:T(8,128)}) fusion(s32[2048]{0:T(1024)S(1)} %get-tuple-element.292, s32[1024]{0:T(1024)S(1)} %dynamic_slice.32, bf16[1,88,2048]{2,1,0:T(8,128)(2,1)S(1)} %get-tuple-element.295, bf16[2,88,16384]{2,1,0:T(8,128)(2,1)} %get-tuple-element.294, s32[]{:T(128)S(6)} %select_n.132), kind=kOutput, calls=%fused_computation.5.clone.1 | convolution fusion | flops 377485312 | bytes 8949764 | tf_op jit(solution)/shard_map/while/body/eval_jaxpr/hdq,hdk->hqk/dot_general | solution.py:68
  178.5 5.0 fusion.50
  183.5 5.5 %fusion.52 = f32[1,88,2048]{2,1,0:T(8,128)S(1)} fusion(f32[1024,2048]{1,0:T(8,128)} %get-tuple-element.259, f32[2048]{0:T(1024)S(1)} %bitcast.105, s32[2048]{0:T(1024)S(1)} %get-tuple-element.292, s32[1024]{0:T(1024)S(1)} %dynamic_slice.32, f32[1,88,2048]{2,1,0:T(8,128)S(1)} %get-tuple-element.278, f32[2048]{0:T(1024)S(1)} %bitcast.112, ...), kind=kOutput, calls=%fused_computation.12.clone.1 | convolution fusion | flops 380125184 | bytes 10039305 | tf_op jit(solution)/shard_map/while/body/eval_jaxpr/hqk,hdk->hdq/dot_general | solution.py:76
  189.1 5.5 %fusion.48 = (f32[2048]{0:T(1024)S(1)}, f32[1024,2048]{1,0:T(8,128)}) fusion(s32[2048]{0:T(1024)S(1)} %get-tuple-element.292, s32[1024]{0:T(1024)S(1)} %dynamic_slice.32, bf16[1,88,2048]{2,1,0:T(8,128)(2,1)S(1)} %get-tuple-element.295, bf16[2,88,16384]{2,1,0:T(8,128)(2,1)} %get-tuple-element.294, s32[]{:T(128)S(6)} %select_n.132), kind=kOutput, calls=%fused_computation.5.clone.1 | convolution fusion | flops 377485312 | bytes 8949764 | tf_op jit(solution)/shard_map/while/body/eval_jaxpr/hdq,hdk->hqk/dot_general | solution.py:68
  199.3 5.4 %fusion.52 = f32[1,88,2048]{2,1,0:T(8,128)S(1)} fusion(f32[1024,2048]{1,0:T(8,128)} %get-tuple-element.259, f32[2048]{0:T(1024)S(1)} %bitcast.105, s32[2048]{0:T(1024)S(1)} %get-tuple-element.292, s32[1024]{0:T(1024)S(1)} %dynamic_slice.32, f32[1,88,2048]{2,1,0:T(8,128)S(1)} %get-tuple-element.278, f32[2048]{0:T(1024)S(1)} %bitcast.112, ...), kind=kOutput, calls=%fused_computation.12.clone.1 | convolution fusion | flops 380125184 | bytes 10039305 | tf_op jit(solution)/shard_map/while/body/eval_jaxpr/hqk,hdk->hdq/dot_general | solution.py:76
  204.7 6.2 %fusion.48 = (f32[2048]{0:T(1024)S(1)}, f32[1024,2048]{1,0:T(8,128)}) fusion(s32[2048]{0:T(1024)S(1)} %get-tuple-element.292, s32[1024]{0:T(1024)S(1)} %dynamic_slice.32, bf16[1,88,2048]{2,1,0:T(8,128)(2,1)S(1)} %get-tuple-element.295, bf16[2,88,16384]{2,1,0:T(8,128)(2,1)} %get-tuple-element.294, s32[]{:T(128)S(6)} %select_n.132), kind=kOutput, calls=%fused_computation.5.clone.1 | convolution fusion | flops 377485312 | bytes 8949764 | tf_op jit(solution)/shard_map/while/body/eval_jaxpr/hdq,hdk->hqk/dot_general | solution.py:68
  215.6 5.6 %fusion.52 = f32[1,88,2048]{2,1,0:T(8,128)S(1)} fusion(f32[1024,2048]{1,0:T(8,128)} %get-tuple-element.259, f32[2048]{0:T(1024)S(1)} %bitcast.105, s32[2048]{0:T(1024)S(1)} %get-tuple-element.292, s32[1024]{0:T(1024)S(1)} %dynamic_slice.32, f32[1,88,2048]{2,1,0:T(8,128)S(1)} %get-tuple-element.278, f32[2048]{0:T(1024)S(1)} %bitcast.112, ...), kind=kOutput, calls=%fused_computation.12.clone.1 | convolution fusion | flops 380125184 | bytes 10039305 | tf_op jit(solution)/shard_map/while/body/eval_jaxpr/hqk,hdk->hdq/dot_general | solution.py:76
  221.2 5.5 %fusion.48 = (f32[2048]{0:T(1024)S(1)}, f32[1024,2048]{1,0:T(8,128)}) fusion(s32[2048]{0:T(1024)S(1)} %get-tuple-element.292, s32[1024]{0:T(1024)S(1)} %dynamic_slice.32, bf16[1,88,2048]{2,1,0:T(8,128)(2,1)S(1)} %get-tuple-element.295, bf16[2,88,16384]{2,1,0:T(8,128)(2,1)} %get-tuple-element.294, s32[]{:T(128)S(6)} %select_n.132), kind=kOutput, calls=%fused_computation.5.clone.1 | convolution fusion | flops 377485312 | bytes 8949764 | tf_op jit(solution)/shard_map/while/body/eval_jaxpr/hdq,hdk->hqk/dot_general | solution.py:68
  226.8 4.9 fusion.50
  231.7 5.7 %fusion.52 = f32[1,88,2048]{2,1,0:T(8,128)S(1)} fusion(f32[1024,2048]{1,0:T(8,128)} %get-tuple-element.259, f32[2048]{0:T(1024)S(1)} %bitcast.105, s32[2048]{0:T(1024)S(1)} %get-tuple-element.292, s32[1024]{0:T(1024)S(1)} %dynamic_slice.32, f32[1,88,2048]{2,1,0:T(8,128)S(1)} %get-tuple-element.278, f32[2048]{0:T(1024)S(1)} %bitcast.112, ...), kind=kOutput, calls=%fused_computation.12.clone.1 | convolution fusion | flops 380125184 | bytes 10039305 | tf_op jit(solution)/shard_map/while/body/eval_jaxpr/hqk,hdk->hdq/dot_general | solution.py:76
  237.4 5.5 %fusion.48 = (f32[2048]{0:T(1024)S(1)}, f32[1024,2048]{1,0:T(8,128)}) fusion(s32[2048]{0:T(1024)S(1)} %get-tuple-element.292, s32[1024]{0:T(1024)S(1)} %dynamic_slice.32, bf16[1,88,2048]{2,1,0:T(8,128)(2,1)S(1)} %get-tuple-element.295, bf16[2,88,16384]{2,1,0:T(8,128)(2,1)} %get-tuple-element.294, s32[]{:T(128)S(6)} %select_n.132), kind=kOutput, calls=%fused_computation.5.clone.1 | convolution fusion | flops 377485312 | bytes 8949764 | tf_op jit(solution)/shard_map/while/body/eval_jaxpr/hdq,hdk->hqk/dot_general | solution.py:68
  242.9 4.9 fusion.50
  247.9 5.7 %fusion.52 = f32[1,88,2048]{2,1,0:T(8,128)S(1)} fusion(f32[1024,2048]{1,0:T(8,128)} %get-tuple-element.259, f32[2048]{0:T(1024)S(1)} %bitcast.105, s32[2048]{0:T(1024)S(1)} %get-tuple-element.292, s32[1024]{0:T(1024)S(1)} %dynamic_slice.32, f32[1,88,2048]{2,1,0:T(8,128)S(1)} %get-tuple-element.278, f32[2048]{0:T(1024)S(1)} %bitcast.112, ...), kind=kOutput, calls=%fused_computation.12.clone.1 | convolution fusion | flops 380125184 | bytes 10039305 | tf_op jit(solution)/shard_map/while/body/eval_jaxpr/hqk,hdk->hdq/dot_general | solution.py:76
  253.6 5.5 %fusion.48 = (f32[2048]{0:T(1024)S(1)}, f32[1024,2048]{1,0:T(8,128)}) fusion(s32[2048]{0:T(1024)S(1)} %get-tuple-element.292, s32[1024]{0:T(1024)S(1)} %dynamic_slice.32, bf16[1,88,2048]{2,1,0:T(8,128)(2,1)S(1)} %get-tuple-element.295, bf16[2,88,16384]{2,1,0:T(8,128)(2,1)} %get-tuple-element.294, s32[]{:T(128)S(6)} %select_n.132), kind=kOutput, calls=%fused_computation.5.clone.1 | convolution fusion | flops 377485312 | bytes 8949764 | tf_op jit(solution)/shard_map/while/body/eval_jaxpr/hdq,hdk->hqk/dot_general | solution.py:68
  263.8 5.4 %fusion.52 = f32[1,88,2048]{2,1,0:T(8,128)S(1)} fusion(f32[1024,2048]{1,0:T(8,128)} %get-tuple-element.259, f32[2048]{0:T(1024)S(1)} %bitcast.105, s32[2048]{0:T(1024)S(1)} %get-tuple-element.292, s32[1024]{0:T(1024)S(1)} %dynamic_slice.32, f32[1,88,2048]{2,1,0:T(8,128)S(1)} %get-tuple-element.278, f32[2048]{0:T(1024)S(1)} %bitcast.112, ...), kind=kOutput, calls=%fused_computation.12.clone.1 | convolution fusion | flops 380125184 | bytes 10039305 | tf_op jit(solution)/shard_map/while/body/eval_jaxpr/hqk,hdk->hdq/dot_general | solution.py:76
  269.2 5.5 %fusion.48 = (f32[2048]{0:T(1024)S(1)}, f32[1024,2048]{1,0:T(8,128)}) fusion(s32[2048]{0:T(1024)S(1)} %get-tuple-element.292, s32[1024]{0:T(1024)S(1)} %dynamic_slice.32, bf16[1,88,2048]{2,1,0:T(8,128)(2,1)S(1)} %get-tuple-element.295, bf16[2,88,16384]{2,1,0:T(8,128)(2,1)} %get-tuple-element.294, s32[]{:T(128)S(6)} %select_n.132), kind=kOutput, calls=%fused_computation.5.clone.1 | convolution fusion | flops 377485312 | bytes 8949764 | tf_op jit(solution)/shard_map/while/body/eval_jaxpr/hdq,hdk->hqk/dot_general | solution.py:68
  279.4 5.4 %fusion.52 = f32[1,88,2048]{2,1,0:T(8,128)S(1)} fusion(f32[1024,2048]{1,0:T(8,128)} %get-tuple-element.259, f32[2048]{0:T(1024)S(1)} %bitcast.105, s32[2048]{0:T(1024)S(1)} %get-tuple-element.292, s32[1024]{0:T(1024)S(1)} %dynamic_slice.32, f32[1,88,2048]{2,1,0:T(8,128)S(1)} %get-tuple-element.278, f32[2048]{0:T(1024)S(1)} %bitcast.112, ...), kind=kOutput, calls=%fused_computation.12.clone.1 | convolution fusion | flops 380125184 | bytes 10039305 | tf_op jit(solution)/shard_map/while/body/eval_jaxpr/hqk,hdk->hdq/dot_general | solution.py:76
  284.9 5.5 %fusion.48 = (f32[2048]{0:T(1024)S(1)}, f32[1024,2048]{1,0:T(8,128)}) fusion(s32[2048]{0:T(1024)S(1)} %get-tuple-element.292, s32[1024]{0:T(1024)S(1)} %dynamic_slice.32, bf16[1,88,2048]{2,1,0:T(8,128)(2,1)S(1)} %get-tuple-element.295, bf16[2,88,16384]{2,1,0:T(8,128)(2,1)} %get-tuple-element.294, s32[]{:T(128)S(6)} %select_n.132), kind=kOutput, calls=%fused_computation.5.clone.1 | convolution fusion | flops 377485312 | bytes 8949764 | tf_op jit(solution)/shard_map/while/body/eval_jaxpr/hdq,hdk->hqk/dot_general | solution.py:68
  295.0 5.4 %fusion.52 = f32[1,88,2048]{2,1,0:T(8,128)S(1)} fusion(f32[1024,2048]{1,0:T(8,128)} %get-tuple-element.259, f32[2048]{0:T(1024)S(1)} %bitcast.105, s32[2048]{0:T(1024)S(1)} %get-tuple-element.292, s32[1024]{0:T(1024)S(1)} %dynamic_slice.32, f32[1,88,2048]{2,1,0:T(8,128)S(1)} %get-tuple-element.278, f32[2048]{0:T(1024)S(1)} %bitcast.112, ...), kind=kOutput, calls=%fused_computation.12.clone.1 | convolution fusion | flops 380125184 | bytes 10039305 | tf_op jit(solution)/shard_map/while/body/eval_jaxpr/hqk,hdk->hdq/dot_general | solution.py:76
  300.5 5.5 %fusion.48 = (f32[2048]{0:T(1024)S(1)}, f32[1024,2048]{1,0:T(8,128)}) fusion(s32[2048]{0:T(1024)S(1)} %get-tuple-element.292, s32[1024]{0:T(1024)S(1)} %dynamic_slice.32, bf16[1,88,2048]{2,1,0:T(8,128)(2,1)S(1)} %get-tuple-element.295, bf16[2,88,16384]{2,1,0:T(8,128)(2,1)} %get-tuple-element.294, s32[]{:T(128)S(6)} %select_n.132), kind=kOutput, calls=%fused_computation.5.clone.1 | convolution fusion | flops 377485312 | bytes 8949764 | tf_op jit(solution)/shard_map/while/body/eval_jaxpr/hdq,hdk->hqk/dot_general | solution.py:68
  310.6 5.4 %fusion.52 = f32[1,88,2048]{2,1,0:T(8,128)S(1)} fusion(f32[1024,2048]{1,0:T(8,128)} %get-tuple-element.259, f32[2048]{0:T(1024)S(1)} %bitcast.105, s32[2048]{0:T(1024)S(1)} %get-tuple-element.292, s32[1024]{0:T(1024)S(1)} %dynamic_slice.32, f32[1,88,2048]{2,1,0:T(8,128)S(1)} %get-tuple-element.278, f32[2048]{0:T(1024)S(1)} %bitcast.112, ...), kind=kOutput, calls=%fused_computation.12.clone.1 | convolution fusion | flops 380125184 | bytes 10039305 | tf_op jit(solution)/shard_map/while/body/eval_jaxpr/hqk,hdk->hdq/dot_general | solution.py:76
  316.1 5.5 %fusion.48 = (f32[2048]{0:T(1024)S(1)}, f32[1024,2048]{1,0:T(8,128)}) fusion(s32[2048]{0:T(1024)S(1)} %get-tuple-element.292, s32[1024]{0:T(1024)S(1)} %dynamic_slice.32, bf16[1,88,2048]{2,1,0:T(8,128)(2,1)S(1)} %get-tuple-element.295, bf16[2,88,16384]{2,1,0:T(8,128)(2,1)} %get-tuple-element.294, s32[]{:T(128)S(6)} %select_n.132), kind=kOutput, calls=%fused_computation.5.clone.1 | convolution fusion | flops 377485312 | bytes 8949764 | tf_op jit(solution)/shard_map/while/body/eval_jaxpr/hdq,hdk->hqk/dot_general | solution.py:68
  326.2 5.4 %fusion.52 = f32[1,88,2048]{2,1,0:T(8,128)S(1)} fusion(f32[1024,2048]{1,0:T(8,128)} %get-tuple-element.259, f32[2048]{0:T(1024)S(1)} %bitcast.105, s32[2048]{0:T(1024)S(1)} %get-tuple-element.292, s32[1024]{0:T(1024)S(1)} %dynamic_slice.32, f32[1,88,2048]{2,1,0:T(8,128)S(1)} %get-tuple-element.278, f32[2048]{0:T(1024)S(1)} %bitcast.112, ...), kind=kOutput, calls=%fused_computation.12.clone.1 | convolution fusion | flops 380125184 | bytes 10039305 | tf_op jit(solution)/shard_map/while/body/eval_jaxpr/hqk,hdk->hdq/dot_general | solution.py:76
  331.7 5.5 %fusion.48 = (f32[2048]{0:T(1024)S(1)}, f32[1024,2048]{1,0:T(8,128)}) fusion(s32[2048]{0:T(1024)S(1)} %get-tuple-element.292, s32[1024]{0:T(1024)S(1)} %dynamic_slice.32, bf16[1,88,2048]{2,1,0:T(8,128)(2,1)S(1)} %get-tuple-element.295, bf16[2,88,16384]{2,1,0:T(8,128)(2,1)} %get-tuple-element.294, s32[]{:T(128)S(6)} %select_n.132), kind=kOutput, calls=%fused_computation.5.clone.1 | convolution fusion | flops 377485312 | bytes 8949764 | tf_op jit(solution)/shard_map/while/body/eval_jaxpr/hdq,hdk->hqk/dot_general | solution.py:68
  341.9 5.4 %fusion.52 = f32[1,88,2048]{2,1,0:T(8,128)S(1)} fusion(f32[1024,2048]{1,0:T(8,128)} %get-tuple-element.259, f32[2048]{0:T(1024)S(1)} %bitcast.105, s32[2048]{0:T(1024)S(1)} %get-tuple-element.292, s32[1024]{0:T(1024)S(1)} %dynamic_slice.32, f32[1,88,2048]{2,1,0:T(8,128)S(1)} %get-tuple-element.278, f32[2048]{0:T(1024)S(1)} %bitcast.112, ...), kind=kOutput, calls=%fused_computation.12.clone.1 | convolution fusion | flops 380125184 | bytes 10039305 | tf_op jit(solution)/shard_map/while/body/eval_jaxpr/hqk,hdk->hdq/dot_general | solution.py:76
  347.3 5.5 %fusion.48 = (f32[2048]{0:T(1024)S(1)}, f32[1024,2048]{1,0:T(8,128)}) fusion(s32[2048]{0:T(1024)S(1)} %get-tuple-element.292, s32[1024]{0:T(1024)S(1)} %dynamic_slice.32, bf16[1,88,2048]{2,1,0:T(8,128)(2,1)S(1)} %get-tuple-element.295, bf16[2,88,16384]{2,1,0:T(8,128)(2,1)} %get-tuple-element.294, s32[]{:T(128)S(6)} %select_n.132), kind=kOutput, calls=%fused_computation.5.clone.1 | convolution fusion | flops 377485312 | bytes 8949764 | tf_op jit(solution)/shard_map/while/body/eval_jaxpr/hdq,hdk->hqk/dot_general | solution.py:68
  357.5 5.4 %fusion.52 = f32[1,88,2048]{2,1,0:T(8,128)S(1)} fusion(f32[1024,2048]{1,0:T(8,128)} %get-tuple-element.259, f32[2048]{0:T(1024)S(1)} %bitcast.105, s32[2048]{0:T(1024)S(1)} %get-tuple-element.292, s32[1024]{0:T(1024)S(1)} %dynamic_slice.32, f32[1,88,2048]{2,1,0:T(8,128)S(1)} %get-tuple-element.278, f32[2048]{0:T(1024)S(1)} %bitcast.112, ...), kind=kOutput, calls=%fused_computation.12.clone.1 | convolution fusion | flops 380125184 | bytes 10039305 | tf_op jit(solution)/shard_map/while/body/eval_jaxpr/hqk,hdk->hdq/dot_general | solution.py:76
  362.9 5.5 %fusion.48 = (f32[2048]{0:T(1024)S(1)}, f32[1024,2048]{1,0:T(8,128)}) fusion(s32[2048]{0:T(1024)S(1)} %get-tuple-element.292, s32[1024]{0:T(1024)S(1)} %dynamic_slice.32, bf16[1,88,2048]{2,1,0:T(8,128)(2,1)S(1)} %get-tuple-element.295, bf16[2,88,16384]{2,1,0:T(8,128)(2,1)} %get-tuple-element.294, s32[]{:T(128)S(6)} %select_n.132), kind=kOutput, calls=%fused_computation.5.clone.1 | convolution fusion | flops 377485312 | bytes 8949764 | tf_op jit(solution)/shard_map/while/body/eval_jaxpr/hdq,hdk->hqk/dot_general | solution.py:68
  373.1 5.4 %fusion.52 = f32[1,88,2048]{2,1,0:T(8,128)S(1)} fusion(f32[1024,2048]{1,0:T(8,128)} %get-tuple-element.259, f32[2048]{0:T(1024)S(1)} %bitcast.105, s32[2048]{0:T(1024)S(1)} %get-tuple-element.292, s32[1024]{0:T(1024)S(1)} %dynamic_slice.32, f32[1,88,2048]{2,1,0:T(8,128)S(1)} %get-tuple-element.278, f32[2048]{0:T(1024)S(1)} %bitcast.112, ...), kind=kOutput, calls=%fused_computation.12.clone.1 | convolution fusion | flops 380125184 | bytes 10039305 | tf_op jit(solution)/shard_map/while/body/eval_jaxpr/hqk,hdk->hdq/dot_general | solution.py:76
  378.5 5.5 %fusion.48 = (f32[2048]{0:T(1024)S(1)}, f32[1024,2048]{1,0:T(8,128)}) fusion(s32[2048]{0:T(1024)S(1)} %get-tuple-element.292, s32[1024]{0:T(1024)S(1)} %dynamic_slice.32, bf16[1,88,2048]{2,1,0:T(8,128)(2,1)S(1)} %get-tuple-element.295, bf16[2,88,16384]{2,1,0:T(8,128)(2,1)} %get-tuple-element.294, s32[]{:T(128)S(6)} %select_n.132), kind=kOutput, calls=%fused_computation.5.clone.1 | convolution fusion | flops 377485312 | bytes 8949764 | tf_op jit(solution)/shard_map/while/body/eval_jaxpr/hdq,hdk->hqk/dot_general | solution.py:68
  388.7 5.4 %fusion.52 = f32[1,88,2048]{2,1,0:T(8,128)S(1)} fusion(f32[1024,2048]{1,0:T(8,128)} %get-tuple-element.259, f32[2048]{0:T(1024)S(1)} %bitcast.105, s32[2048]{0:T(1024)S(1)} %get-tuple-element.292, s32[1024]{0:T(1024)S(1)} %dynamic_slice.32, f32[1,88,2048]{2,1,0:T(8,128)S(1)} %get-tuple-element.278, f32[2048]{0:T(1024)S(1)} %bitcast.112, ...), kind=kOutput, calls=%fused_computation.12.clone.1 | convolution fusion | flops 380125184 | bytes 10039305 | tf_op jit(solution)/shard_map/while/body/eval_jaxpr/hqk,hdk->hdq/dot_general | solution.py:76
  394.1 5.5 %fusion.48 = (f32[2048]{0:T(1024)S(1)}, f32[1024,2048]{1,0:T(8,128)}) fusion(s32[2048]{0:T(1024)S(1)} %get-tuple-element.292, s32[1024]{0:T(1024)S(1)} %dynamic_slice.32, bf16[1,88,2048]{2,1,0:T(8,128)(2,1)S(1)} %get-tuple-element.295, bf16[2,88,16384]{2,1,0:T(8,128)(2,1)} %get-tuple-element.294, s32[]{:T(128)S(6)} %select_n.132), kind=kOutput, calls=%fused_computation.5.clone.1 | convolution fusion | flops 377485312 | bytes 8949764 | tf_op jit(solution)/shard_map/while/body/eval_jaxpr/hdq,hdk->hqk/dot_general | solution.py:68
  404.3 5.4 %fusion.52 = f32[1,88,2048]{2,1,0:T(8,128)S(1)} fusion(f32[1024,2048]{1,0:T(8,128)} %get-tuple-element.259, f32[2048]{0:T(1024)S(1)} %bitcast.105, s32[2048]{0:T(1024)S(1)} %get-tuple-element.292, s32[1024]{0:T(1024)S(1)} %dynamic_slice.32, f32[1,88,2048]{2,1,0:T(8,128)S(1)} %get-tuple-element.278, f32[2048]{0:T(1024)S(1)} %bitcast.112, ...), kind=kOutput, calls=%fused_computation.12.clone.1 | convolution fusion | flops 380125184 | bytes 10039305 | tf_op jit(solution)/shard_map/while/body/eval_jaxpr/hqk,hdk->hdq/dot_general | solution.py:76
  409.8 5.5 %fusion.48 = (f32[2048]{0:T(1024)S(1)}, f32[1024,2048]{1,0:T(8,128)}) fusion(s32[2048]{0:T(1024)S(1)} %get-tuple-element.292, s32[1024]{0:T(1024)S(1)} %dynamic_slice.32, bf16[1,88,2048]{2,1,0:T(8,128)(2,1)S(1)} %get-tuple-element.295, bf16[2,88,16384]{2,1,0:T(8,128)(2,1)} %get-tuple-element.294, s32[]{:T(128)S(6)} %select_n.132), kind=kOutput, calls=%fused_computation.5.clone.1 | convolution fusion | flops 377485312 | bytes 8949764 | tf_op jit(solution)/shard_map/while/body/eval_jaxpr/hdq,hdk->hqk/dot_general | solution.py:68
  419.9 5.4 %fusion.52 = f32[1,88,2048]{2,1,0:T(8,128)S(1)} fusion(f32[1024,2048]{1,0:T(8,128)} %get-tuple-element.259, f32[2048]{0:T(1024)S(1)} %bitcast.105, s32[2048]{0:T(1024)S(1)} %get-tuple-element.292, s32[1024]{0:T(1024)S(1)} %dynamic_slice.32, f32[1,88,2048]{2,1,0:T(8,128)S(1)} %get-tuple-element.278, f32[2048]{0:T(1024)S(1)} %bitcast.112, ...), kind=kOutput, calls=%fused_computation.12.clone.1 | convolution fusion | flops 380125184 | bytes 10039305 | tf_op jit(solution)/shard_map/while/body/eval_jaxpr/hqk,hdk->hdq/dot_general | solution.py:76
  426.3 6.4 %all-to-all-start = ((bf16[88,16,128]{2,0,1:T(8,128)(2,1)}), bf16[88,16,128]{2,0,1:T(8,128)(2,1)S(1)}, u32[]{:S(2)}, u32[]{:S(2)}) async-start(bf16[88,16,128]{2,0,1:T(8,128)(2,1)} %copy.35), calls=%async_computation | async-start | bytes 720896 | tf_op jit(solution)/shard_map/all_to_all | solution.py:105
  432.8 7.6 %convert_element_type.50 = f32[1408,2048]{0,1:T(8,128)} convert(bf16[1408,2048]{0,1:T(8,128)(2,1)} %copy.37) | non-fusion elementwise | flops 2883584 | bytes 17301504 | tf_op jit(solution)/shard_map/convert_element_type | solution.py:36
  446.1 8.8 %fusion.27 = bf16[32,1408]{1,0:T(8,128)(2,1)} fusion(bf16[4,1408,1408]{2,1,0:T(8,128)(2,1)} %all-gather.9.cloned.1.call-done, bf16[1408,32,4]{0,2,1:T(4,128)(2,1)S(1)} %reshape.212), kind=kOutput, calls=%fused_computation.37 | convolution fusion | flops 507555840 | bytes 16310272 | tf_op jit(solution)/shard_map/fgi,ifd->gd/dot_general | solution.py:121
  456.4 41.4 %all-gather.11.cloned.1.call-done = bf16[512,1408]{1,0:T(8,128)(2,1)} async-done(((bf16[32,1408]{1,0:T(8,128)(2,1)}), bf16[512,1408]{1,0:T(8,128)(2,1)}) %all-gather.11.cloned.1.call-update) | async-done | bytes 1441808 | tf_op jit(solution)/shard_map/all_gather | solution.py:122
  (131 shorter events, 91.2 us)
Async XLA Ops:
  6.5 110.4 %copy-start = (bf16[2,88,1408]{2,1,0:T(8,128)(2,1)S(1)}, bf16[2,88,1408]{2,1,0:T(8,128)(2,1)}, u32[]{:S(2)}) copy-start(bf16[2,88,1408]{2,1,0:T(8,128)(2,1)} %param.16) | copy-start | bytes 1486852
  6.5 82.5 %all-gather.5.cloned.1.call-start = ((), (), s32[]{:S(2)}) async-start(), calls=%async_computation.1 | async-start | bytes 10340352 | tf_op jit(solution)/shard_map/all_gather | solution.py:32
  8.6 157.4 %all-gather.7.cloned.1.call-start = ((), (), s32[]{:S(2)}) async-start(), calls=%async_computation.2 | async-start | bytes 6782976 | tf_op jit(solution)/shard_map/all_gather | solution.py:59
  103.5 4.5 copy-start.2
  111.9 14.4 %copy-start.4 = (bf16[88,1408]{1,0:T(8,128)(2,1)S(1)}, bf16[88,1408]{1,0:T(8,128)(2,1)}, u32[]{:S(2)}) copy-start(bf16[88,1408]{1,0:T(8,128)(2,1)} %param.15) | copy-start | bytes 743428
  126.1 320.0 %all-gather.9.cloned.1.call-start = ((), (), s32[]{:S(2)}) async-start(), calls=%async_computation.3 | async-start | bytes 16850944 | tf_op jit(solution)/shard_map/all_gather | solution.py:119
  126.4 46.4 %copy-start.3 = (s32[2048]{0:T(1024)S(1)}, s32[2048]{0:T(1024)}, u32[]{:S(2)}) copy-start(s32[2048]{0:T(1024)} %param.19) | copy-start | bytes 24580
  172.7 260.0 %copy-start.5 = (bf16[1408]{0:T(1024)(128)(2,1)S(1)}, bf16[1408]{0:T(1024)(128)(2,1)}, u32[]{:S(2)}) copy-start(bf16[1408]{0:T(1024)(128)(2,1)} %param.21) | copy-start | bytes 8452
  426.3 16.2 %all-to-all-start = ((bf16[88,16,128]{2,0,1:T(8,128)(2,1)}), bf16[88,16,128]{2,0,1:T(8,128)(2,1)S(1)}, u32[]{:S(2)}, u32[]{:S(2)}) async-start(bf16[88,16,128]{2,0,1:T(8,128)(2,1)} %copy.35), calls=%async_computation | async-start | bytes 720896 | tf_op jit(solution)/shard_map/all_to_all | solution.py:105
  432.7 65.0 %all-gather.11.cloned.1.call-start = ((), (), s32[]{:S(2)}) async-start(), calls=%async_computation.4 | async-start | bytes 1531904 | tf_op jit(solution)/shard_map/all_gather | solution.py:122
  446.0 55.1 %copy-start.1 = (bf16[2,88,1408]{2,1,0:T(8,128)(2,1)S(1)}, bf16[2,88,1408]{2,1,0:T(8,128)(2,1)}, u32[]{:S(2)}) copy-start(bf16[2,88,1408]{2,1,0:T(8,128)(2,1)} %param.16) | copy-start | bytes 1486852
Sparse Core Ops, SparseCore 0:
  9.5 79.4 all-gather.4
  126.2 39.7 all-gather.6
  168.2 106.3 all-gather.8
  455.1 42.6 all-gather.10
